TPU v7x, 32 devices: a whole 2x2x4 slice. The times are simulated.
32 devices in a mesh: vx: 2 (over x), vy: 4 (over y, core), scan: 4 (over z).
Axes of the slice: x: 2, y: 2, z: 4, core: 2. Of those that a mesh axis runs over, the one named last changes fastest.
Arguments:
- volume: bfloat16 [2, 64, 256, 256], P(None, 'vx', 'vy'), may hold values from -6 to 6
- tile_matrix: bfloat16 [4, 2, 8, 1024, 128], P('scan', 'vx', 'vy'), may hold values from -0.09375 to 0.09375
- tile_offset: int32 [4, 2, 8], P('scan', 'vx', 'vy'), may hold values from 0 to 384
- patch_count: int32 [4, 8], P('scan', ('vx', 'vy')), may hold values from 1 to 3, as said below
- scan_position: int32 [4, 8, 3, 2], P('scan', ('vx', 'vy')), may hold values from 0 to 256, as said below
- measured: float32 [4, 8, 3, 256, 256], P('scan', ('vx', 'vy')), may hold values from 0.2 to 5
- illumination: float32 [2, 256, 256], replicated, may hold values from -6 to 6
Outputs:
- change: float32 [2, 64, 256, 256], P(None, 'vx', 'vy', 'scan')
Inputs may be any that keep to these rules, and one draw needn't show every extreme that they name: `patch_count`: an owner's slots below its count hold measured patches, the others are unused; at every angle some owner holds 3. `scan_position`: column 0 is a patch's first detector column, 0 to 256; column 1 its first row, 0 to 0.
All inputs are finite; a program needn't handle non-finite values.
Results may differ from a plain program's by a relative error of at most 0.0085.
Values may be sent and summed in bfloat16 or wider, within the bound.
No kernel may reach another device: no remote copies, remote signals or barrier semaphores. Data moves between devices by JAX's collectives and lax.ppermute only.
A program may use at most 64 MiB of HBM per device.

v0:
```python
import math
import jax
import jax.numpy as jnp
from jax import lax
from jax.sharding import PartitionSpec as P

TILE = 32
NZ = 256
U = 512
TU = 128
PATCH_SIDE = 256
ABSORPTION = 0.2
STEP_LENGTH = 0.003


def dft_tables(length):
    counter = jnp.arange(length, dtype=jnp.int32)
    product = counter[:, None] * counter[None, :] % length
    radians = product.astype(jnp.float32) * (2.0 * math.pi / length)
    scaling = 1.0 / math.sqrt(length)
    return (jnp.cos(radians) * scaling, jnp.sin(radians) * scaling)


def matmul(left, right):
    return jnp.dot(left, right, precision=lax.Precision.HIGHEST)


def patch_misfit(window, illumination, intensity, cosine_table, sine_table):
    amplitude = jnp.exp(-ABSORPTION * window[1])
    trans_re = amplitude * jnp.cos(window[0])
    trans_im = amplitude * jnp.sin(window[0])
    exit_re = illumination[0] * trans_re - illumination[1] * trans_im
    exit_im = illumination[0] * trans_im + illumination[1] * trans_re
    half_re = matmul(cosine_table, exit_re) + matmul(sine_table, exit_im)
    half_im = matmul(cosine_table, exit_im) - matmul(sine_table, exit_re)
    far_re = matmul(half_re, cosine_table) + matmul(half_im, sine_table)
    far_im = matmul(half_im, cosine_table) - matmul(half_re, sine_table)
    residue = far_re * far_re + far_im * far_im - intensity
    return jnp.sum(residue * residue)


def place_patch(summed_total, slope, corner):
    anchor = (jnp.zeros((), jnp.int32), corner[0], corner[1])
    before = lax.dynamic_slice(summed_total, anchor, slope.shape)
    return lax.dynamic_update_slice(summed_total, before + slope, anchor)


def patch_term(
    summed_total, projected_field, corner, intensity, illumination, cosine_table, sine_table
):
    anchor = (jnp.zeros((), jnp.int32), corner[0], corner[1])
    window = lax.dynamic_slice(projected_field, anchor, (2, PATCH_SIDE, PATCH_SIDE))
    slope = jax.grad(patch_misfit)(window, illumination, intensity, cosine_table, sine_table)
    return place_patch(summed_total, slope, corner)


def brick_tiles(field):
    components, width_x, width_y, depth_cells = field.shape
    blocks = field.reshape(components, width_x // TILE, TILE, width_y // TILE, TILE, depth_cells)
    blocks = blocks.transpose(1, 3, 0, 2, 4, 5)
    return blocks.reshape(-1, components, TILE * TILE, depth_cells)


def tiles_brick(blocks, width_x, width_y):
    components = blocks.shape[1]
    depth_cells = blocks.shape[3]
    shaped = blocks.reshape(width_x // TILE, width_y // TILE, components, TILE, TILE, depth_cells)
    return shaped.transpose(2, 0, 3, 1, 4, 5).reshape(components, width_x, width_y, depth_cells)


def partial_projection(current, matrices, offsets):
    blocks = brick_tiles(current)
    tile_parts = jnp.einsum("tku,tckz->tcuz", matrices, blocks, preferred_element_type=jnp.float32)
    summed_total = jnp.zeros((2, U, NZ), jnp.float32)
    for tile_index in range(tile_parts.shape[0]):
        anchor = (jnp.zeros((), jnp.int32), offsets[tile_index], jnp.zeros((), jnp.int32))
        before = lax.dynamic_slice(summed_total, anchor, tile_parts.shape[1:])
        summed_total = lax.dynamic_update_slice(
            summed_total, before + tile_parts[tile_index], anchor
        )
    return summed_total


def cut_windows(image, offsets):

    def cut_window(offset):
        anchor = (jnp.zeros((), jnp.int32), offset, jnp.zeros((), jnp.int32))
        return lax.dynamic_slice(image, anchor, (2, TU, NZ))

    return jax.vmap(cut_window)(offsets)


def back_tiles(matrices, windows, width_x, width_y):
    blocks = jnp.einsum("tku,tcuz->tckz", matrices, windows, preferred_element_type=jnp.float32)
    return tiles_brick(blocks, width_x, width_y)


def per_device(
    volume, tile_matrix, tile_offset, patch_count, scan_position, measured, illumination
):
    cosine_table, sine_table = dft_tables(PATCH_SIDE)
    matrices = tile_matrix[0].reshape(-1, TILE * TILE, TU)
    offsets = tile_offset[0].reshape(-1)
    live_count = patch_count[0, 0]
    positions = scan_position[0, 0]
    intensity_values = measured[0, 0]
    width_x = volume.shape[1]
    width_y = volume.shape[2]
    slab_depth = NZ // lax.axis_size("scan")
    slab_start = lax.axis_index("scan") * slab_depth

    def own_slot(slot_index, running, projected_field):
        return patch_term(
            running,
            projected_field,
            positions[slot_index],
            intensity_values[slot_index],
            illumination,
            cosine_table,
            sine_table,
        )

    iterate = lax.dynamic_slice_in_dim(volume, slab_start, slab_depth, 3).astype(jnp.float32)
    projected_field = lax.psum(partial_projection(volume, matrices, offsets), ("vx", "vy"))
    image = lax.psum(
        lax.fori_loop(
            0,
            live_count,
            lambda slot_index, running: own_slot(slot_index, running, projected_field),
            jnp.zeros_like(projected_field),
        ),
        ("vx", "vy"),
    )
    windows = cut_windows(image, offsets).astype(jnp.bfloat16)
    slope = back_tiles(matrices, windows, width_x, width_y)
    slope_sum = lax.psum_scatter(
        slope.astype(jnp.bfloat16), "scan", scatter_dimension=3, tiled=True
    ).astype(jnp.float32)
    iterate = iterate - STEP_LENGTH * slope_sum
    return iterate - lax.dynamic_slice_in_dim(volume, slab_start, slab_depth, 3).astype(jnp.float32)


def solution(mesh):
    in_specs = (
        P(None, "vx", "vy", None),
        P("scan", "vx", "vy", None, None),
        P("scan", "vx", "vy"),
        P("scan", ("vx", "vy")),
        P("scan", ("vx", "vy"), None, None),
        P("scan", ("vx", "vy"), None, None, None),
        P(),
    )
    out_specs = P(None, "vx", "vy", "scan")
    return jax.shard_map(
        per_device, mesh=mesh, in_specs=in_specs, out_specs=out_specs, check_vma=False
    )
```

profile of v0, /device:TPU:0, one launch (start us, length us, event | category | flops | bytes accessed | tf_op | source)
XLA Modules:
  0.0 327.8 jit_solution(10603027786342075903)
XLA Ops:
  6.5 1.3 fusion.124
  10.4 1.8 copy.25
  12.2 1.0 convolution_bitcast_fusion
  14.5 0.1 broadcast.46
  14.7 1.6 dynamic_update_slice.10
  16.3 0.1 fusion.117
  16.5 1.6 dynamic_update_slice.11
  18.1 1.0 copy-done.3
  19.2 0.2 copy.27
  19.4 59.3 %all-reduce.6.cloned.1.call-done = f32[2,512,256]{1,2,0:T(8,128)} async-done(((f32[2,512,256]{1,2,0:T(8,128)}), f32[2,512,256]{1,2,0:T(8,128)}) %all-reduce.6.cloned.1.call-update) | async-done | bytes 1048592 | tf_op jit(solution)/shard_map/psum | solution.py:124
  78.7 1.2 broadcast.46.clone
  79.9 51.8 %while.12 = (s32[]{:T(128)}, f32[2,512,256]{2,0,1:T(2,128)}, s32[]{:T(128)}, s32[3,2]{0,1:T(2,128)S(1)}, f32[2,512,256]{1,2,0:T(8,128)}, /*index=5*/f32[2,256,25...) while((s32[]{:T(128)}, f32[2,512,256]{2,0,1:T(2,128)}, ...), condition=%wide.region_2.3_spmd.clone.clone, body=%wide.region_1.2_spmd.clone.clone.sunk | while | flops 3240427520 | bytes 30671164 | solution.py:126
  98.5 0.1 constant_dynamic-slice_fusion.4
  98.6 0.5 slice.79
  101.0 2.2 fusion.184
  103.2 1.4 fusion.185
  104.6 1.4 convolution_subtract_fusion.4
  106.0 1.5 fusion.186
  107.4 1.4 fusion.187
  108.8 1.4 convolution_add_fusion.9
  110.2 1.5 convolution_subtract_fusion.5
  111.7 1.5 fusion.188
  113.1 2.4 add_multiply_fusion.3
  115.6 1.4 fusion.191
  117.0 1.4 convolution_add_fusion.11
  118.3 1.4 fusion.189
  119.7 1.4 convolution_add_fusion.10
  121.1 1.5 fusion.190
  122.6 1.5 fusion.192
  124.1 1.5 fusion.193
  125.5 2.4 fusion.194
  128.0 1.2 fusion.195
  129.2 0.2 constant_dynamic-slice_fusion.5
  129.4 0.2 copy.43
  129.6 0.1 add_add_fusion.2
  129.7 0.2 copy.44
  129.9 1.0 constant_dynamic-update-slice_fusion.2
  131.7 112.3 %all-reduce.7 = bf16[2,512,256]{2,0,1:T(2,128)(2,1)S(1)} all-reduce(f32[2,512,256]{2,0,1:T(2,128)} %get-tuple-element.94), channel_id=1, replica_groups=mesh['vx'=2,'vy'=4,'scan'=4] {'vx','vy'}, use_global_device_ids=true, to_apply=%region_3.4 | all-reduce | flops 262144 | bytes 1572864 | tf_op jit(solution)/shard_map/psum | solution.py:125
  244.1 1.1 gather_fusion
  245.1 0.8 convert_bitcast_fusion
  245.9 2.6 copy.30
  248.5 1.8 copy.31
  250.3 6.7 %copy.34 = bf16[2,32,64,256]{2,1,0,3:T(8,128)(2,1)} copy(bf16[2,32,64,256]{3,2,1,0:T(8,128)(2,1)S(1)} %bitcast.209) | data formatting | bytes 4194304
  257.0 6.6 %reshape.60 = bf16[256,4096]{1,0:T(8,128)(2,1)} reshape(bf16[256,2,32,64]{3,2,1,0:T(8,128)(2,1)} %bitcast.208) | data formatting | bytes 4194304
  263.6 48.2 %reduce-scatter.4.cloned.1.call-done = bf16[64,4096]{1,0:T(8,128)(2,1)} async-done(((bf16[256,4096]{1,0:T(8,128)(2,1)}), bf16[64,4096]{1,0:T(8,128)(2,1)}) %reduce-scatter.4.cloned.1.call-update) | async-done | bytes 524304
  311.8 2.7 reshape.61
  314.6 2.9 copy.35
  317.5 3.1 subtract_subtract_fusion
  (21 shorter events, 0.1 us)
Async XLA Ops:
  6.5 5.7 %copy-start = (bf16[1,1,2,1024,128]{4,3,2,1,0:T(8,128)(2,1)S(1)}, bf16[1,1,2,1024,128]{4,3,2,1,0:T(8,128)(2,1)}, u32[]{:S(2)}) copy-start(bf16[1,1,2,1024,128]{4,3,2,1,0:T(8,128)(2,1)} %param.10) | copy-start | bytes 1572868
  6.5 72.2 %all-reduce.6.cloned.1.call-start = ((), (), s32[]{:S(2)}) async-start(), calls=%async_computation.1 | async-start | bytes 2097152 | tf_op jit(solution)/shard_map/psum | solution.py:124
  13.2 6.0 %copy-start.5 = (f32[2,256,256]{2,1,0:T(8,128)S(1)}, f32[2,256,256]{2,1,0:T(8,128)}, u32[]{:S(2)}) copy-start(f32[2,256,256]{2,1,0:T(8,128)} %param.15) | copy-start | bytes 1572868
  14.7 4.7 %copy-start.7 = (s32[1,1,2]{2,1,0:T(1,128)S(1)}, s32[1,1,2]{2,1,0:T(1,128)}, u32[]{:S(2)}) copy-start(s32[1,1,2]{2,1,0:T(1,128)} %param.11) | copy-start | bytes 28
  16.3 63.6 %copy-start.6 = (s32[1,1,3,2]{2,3,1,0:T(2,128)S(1)}, s32[1,1,3,2]{2,3,1,0:T(2,128)}, u32[]{:S(2)}) copy-start(s32[1,1,3,2]{2,3,1,0:T(2,128)} %param.13) | copy-start | bytes 76
  18.1 1.0 copy-start.3
  19.1 292.7 %reduce-scatter.4.cloned.1.call-start = ((), (), s32[]{:S(2)}) async-start(), calls=%async_computation.2 | async-start | bytes 2621440
  121.1 4.4 %copy-start.1 = (f32[2,512,256]{1,2,0:T(8,128)S(1)}, f32[2,512,256]{1,2,0:T(8,128)}, u32[]{:S(2)}) copy-start(f32[2,512,256]{1,2,0:T(8,128)} %get-tuple-element.294) | copy-start | bytes 3145732 | tf_op jit(solution)/shard_map/while
  125.5 3.6 %copy-start.2 = (f32[2,512,256]{2,0,1:T(2,128)S(1)}, f32[2,512,256]{2,0,1:T(2,128)}, u32[]{:S(2)}) copy-start(f32[2,512,256]{2,0,1:T(2,128)} %get-tuple-element.279) | copy-start | bytes 3145732 | tf_op jit(solution)/shard_map/while
  263.6 53.9 %copy-start.4 = (bf16[2,32,64,256]{3,2,1,0:T(8,128)(2,1)S(1)}, bf16[2,32,64,256]{3,2,1,0:T(8,128)(2,1)}, u32[]{:S(2)}) copy-start(bf16[2,32,64,256]{3,2,1,0:T(8,128)(2,1)} %param.9) | copy-start | bytes 6291460
Sparse Core Ops, SparseCore 0:
  19.2 59.4 all-reduce.5
  263.7 48.0 reduce-scatter.3
where the time goes:
time: 331 us; the launch traced here: 328 us
  blocking collectives  112 us (34%)
  waiting for transfers between devices  107 us (32%)
  local copies, waits for them, and re-layouts  35.6 us (11%)
  matrix products  26.3 us (8%)
  loops' own time  21.5 us (6%)
  between operations  17.9 us (5%)
  other arithmetic  6.69 us (2%)
    psum x1, blocking collectives, per_device(): lax.psum(lax.fori_loop(0, live_count, lambda slot_index, running: own_slo...  112 us
    psum x1, waiting for transfers between devices, per_device(): lax.psum(partial_projection(volume, matrices, offsets), ('vx', 'vy'))  59.3 us
    unnamed x3, waiting for transfers between devices  48.2 us
    dot_general x16, matrix products, matmul(): return jnp.dot(left, right, precision=lax.Precision.HIGHEST)  24.6 us
    another operation x1, loops' own time, per_device(): lax.fori_loop(0, live_count, lambda slot_index, running: own_slot(slot_in...  21.5 us
    unnamed x17, local copies, waits for them, and re-layouts  20.1 us
  transfers between devices with their start and end apart: 2, of which 2 were waited for; matrix products, arithmetic and copies ran while one was open for 0% of the time, Pallas kernels for 0%

commit v1 on v0

--- a/solution.py
+++ b/solution.py
@@ -122,14 +122,17 @@
 
     iterate = lax.dynamic_slice_in_dim(volume, slab_start, slab_depth, 3).astype(jnp.float32)
     projected_field = lax.psum(partial_projection(volume, matrices, offsets), ("vx", "vy"))
-    image = lax.psum(
-        lax.fori_loop(
-            0,
-            live_count,
-            lambda slot_index, running: own_slot(slot_index, running, projected_field),
-            jnp.zeros_like(projected_field),
+    image = jnp.sum(
+        lax.all_gather(
+            lax.fori_loop(
+                0,
+                live_count,
+                lambda slot_index, running: own_slot(slot_index, running, projected_field),
+                jnp.zeros_like(projected_field),
+            ),
+            ("vx", "vy"),
         ),
-        ("vx", "vy"),
+        axis=0,
     )
     windows = cut_windows(image, offsets).astype(jnp.bfloat16)
     slope = back_tiles(matrices, windows, width_x, width_y)

time: 331 us -> 344 us (1.039)
  waiting for transfers between devices: 107 us -> 227 us
  blocking collectives: 112 us -> 0 us
  other arithmetic: 6.69 us -> 10.7 us
    all_gather x0 -> x1, waiting for transfers between devices: none -> 124 us  [per_device(): lax.all_gather(lax.fori_loop(0, live_count, lambda slot_index, running: o...]
    psum x1 -> x0, blocking collectives: 112 us -> none  [per_device(): lax.psum(lax.fori_loop(0, live_count, lambda slot_index, running: own_slo...]
    unnamed x3 -> x4, waiting for transfers between devices: 48.2 us -> 43.8 us
    reduce_sum x0 -> x1, other arithmetic: none -> 4 us  [per_device(): jnp.sum(lax.all_gather(lax.fori_loop(0, live_count, lambda slot_index, ru...]
  transfers between devices with their start and end apart: 2 -> 3, of which waited for: 2 -> 3; matrix products, arithmetic and copies ran while one was open for 0% -> 0% of each run, Pallas kernels for 0% -> 0%
where the time goes in v1:
time: 344 us; the launch traced here: 341 us
  waiting for transfers between devices  227 us (66%)
  local copies, waits for them, and re-layouts  38.1 us (11%)
  matrix products  26.3 us (8%)
  loops' own time  21.1 us (6%)
  between operations  17.3 us (5%)
  other arithmetic  10.7 us (3%)
    all_gather x1, waiting for transfers between devices, per_device(): lax.all_gather(lax.fori_loop(0, live_count, lambda slot_index, running: o...  124 us
    psum x1, waiting for transfers between devices, per_device(): lax.psum(partial_projection(volume, matrices, offsets), ('vx', 'vy'))  59.3 us
    unnamed x4, waiting for transfers between devices  43.8 us
    dot_general x16, matrix products, matmul(): return jnp.dot(left, right, precision=lax.Precision.HIGHEST)  24.6 us
    another operation x1, loops' own time, per_device(): lax.fori_loop(0, live_count, lambda slot_index, running: own_slot(slot_in...  21.1 us
    unnamed x17, local copies, waits for them, and re-layouts  20.2 us
  transfers between devices with their start and end apart: 3, of which 3 were waited for; matrix products, arithmetic and copies ran while one was open for 0% of the time, Pallas kernels for 0%

profile of v1, /device:TPU:0, one launch (start us, length us, event | category | flops | bytes accessed | tf_op | source)
XLA Modules:
  0.0 340.6 jit_solution(14666625585717177067)
XLA Ops:
  6.5 1.3 fusion.124
  10.3 1.8 copy.22
  12.1 1.0 convolution_bitcast_fusion
  14.3 0.1 broadcast.46
  14.5 1.6 dynamic_update_slice.10
  16.1 0.1 fusion.117
  16.3 1.6 dynamic_update_slice.11
  17.9 1.0 copy-done.3
  19.0 0.2 copy.24
  19.2 59.3 %all-reduce.5.cloned.1.call-done = f32[2,512,256]{1,2,0:T(8,128)} async-done(((f32[2,512,256]{1,2,0:T(8,128)}), f32[2,512,256]{1,2,0:T(8,128)}) %all-reduce.5.cloned.1.call-update) | async-done | bytes 1048592 | tf_op jit(solution)/shard_map/psum | solution.py:124
  78.5 1.0 broadcast.46.clone
  79.5 53.7 %while.12 = (s32[]{:T(128)}, f32[2,512,256]{2,1,0:T(8,128)}, s32[]{:T(128)}, s32[3,2]{0,1:T(2,128)S(1)}, f32[2,512,256]{1,2,0:T(8,128)}, /*index=5*/f32[2,256,25...) while((s32[]{:T(128)}, f32[2,512,256]{2,1,0:T(8,128)}, ...), condition=%wide.region_2.3_spmd.clone.clone, body=%wide.region_1.2_spmd.clone.clone.sunk | while | flops 3240427520 | bytes 30671164 | solution.py:127
  98.0 0.5 slice.79
  100.2 2.2 fusion.184
  102.4 1.4 fusion.185
  103.8 1.4 convolution_subtract_fusion.4
  105.2 1.5 fusion.186
  106.6 1.4 fusion.187
  108.0 1.4 convolution_add_fusion.9
  109.4 1.5 convolution_subtract_fusion.5
  110.9 1.5 fusion.188
  112.3 2.4 add_multiply_fusion.3
  114.8 1.4 fusion.191
  116.2 1.4 convolution_add_fusion.11
  117.5 1.4 fusion.189
  118.9 1.4 convolution_add_fusion.10
  120.3 1.5 fusion.190
  121.8 1.5 fusion.192
  123.2 1.5 fusion.193
  124.7 2.4 fusion.194
  127.2 1.2 fusion.195
  128.4 0.2 copy.45
  128.6 0.1 add_add_fusion.2
  128.7 0.2 copy.46
  128.9 3.4 %dynamic_update_slice.15 = f32[2,512,256]{2,1,0:T(8,128)} dynamic-update-slice(f32[2,512,256]{2,1,0:T(8,128)} %get-tuple-element.279, f32[2,256,256]{2,1,0:T(8,128)S(1)} %copy.46, s32[]{:T(128)} %constant.22.clone.1..sunk, s32[]{:T(128)S(6)} %select_n.158, s32[]{:T(128)} %constant.22.clone.1..sunk) | dynamic-update-slice | bytes 1048580 | tf_op jit(solution)/shard_map/while/body/dynamic_update_slice | solution.py:45
  133.3 123.8 %all-gather.3.cloned.1.call-done = f32[16,512,256]{2,1,0:T(8,128)} async-done(((f32[2,512,256]{2,1,0:T(8,128)}), f32[16,512,256]{2,1,0:T(8,128)}) %all-gather.3.cloned.1.call-update) | async-done | bytes 8388624 | tf_op jit(solution)/shard_map/all_gather | solution.py:126
  257.1 4.0 %reduce_sum.9 = bf16[2,512,256]{2,1,0:T(8,128)(2,1)S(1)} reduce(f32[8,2,512,256]{3,2,1,0:T(8,128)} %bitcast.211, f32[]{:T(128)} %constant.26.clone.1), dimensions={0}, to_apply=%region_3.4 | reduce | flops 1835008 | bytes 8912900 | tf_op jit(solution)/shard_map/reduce_sum | solution.py:125
  261.1 0.5 copy.27
  261.6 1.1 gather_fusion
  262.7 0.8 convert_bitcast_fusion
  263.4 2.6 copy.29
  266.0 1.8 copy.30
  267.8 6.7 %copy.33 = bf16[2,32,64,256]{2,1,0,3:T(8,128)(2,1)} copy(bf16[2,32,64,256]{3,2,1,0:T(8,128)(2,1)S(1)} %bitcast.210) | data formatting | bytes 4194304
  274.5 6.6 %reshape.61 = bf16[256,4096]{1,0:T(8,128)(2,1)} reshape(bf16[256,2,32,64]{3,2,1,0:T(8,128)(2,1)} %bitcast.209) | data formatting | bytes 4194304
  281.2 43.8 %reduce-scatter.4.cloned.1.call-done = bf16[64,4096]{1,0:T(8,128)(2,1)} async-done(((bf16[256,4096]{1,0:T(8,128)(2,1)}), bf16[64,4096]{1,0:T(8,128)(2,1)}) %reduce-scatter.4.cloned.1.call-update) | async-done | bytes 524304
  324.9 2.7 reshape.62
  327.7 2.9 copy.34
  330.6 3.1 subtract_subtract_fusion
  (25 shorter events, 0.3 us)
Async XLA Ops:
  6.5 5.5 %copy-start = (bf16[1,1,2,1024,128]{4,3,2,1,0:T(8,128)(2,1)S(1)}, bf16[1,1,2,1024,128]{4,3,2,1,0:T(8,128)(2,1)}, u32[]{:S(2)}) copy-start(bf16[1,1,2,1024,128]{4,3,2,1,0:T(8,128)(2,1)} %param.10) | copy-start | bytes 1572868
  6.5 71.9 %all-reduce.5.cloned.1.call-start = ((), (), s32[]{:S(2)}) async-start(), calls=%async_computation.1 | async-start | bytes 2097152 | tf_op jit(solution)/shard_map/psum | solution.py:124
  13.0 5.9 %copy-start.5 = (f32[2,256,256]{2,1,0:T(8,128)S(1)}, f32[2,256,256]{2,1,0:T(8,128)}, u32[]{:S(2)}) copy-start(f32[2,256,256]{2,1,0:T(8,128)} %param.15) | copy-start | bytes 1572868
  16.1 63.4 %copy-start.6 = (s32[1,1,3,2]{2,3,1,0:T(2,128)S(1)}, s32[1,1,3,2]{2,3,1,0:T(2,128)}, u32[]{:S(2)}) copy-start(s32[1,1,3,2]{2,3,1,0:T(2,128)} %param.13) | copy-start | bytes 76
  17.9 1.0 copy-start.3
  18.9 238.2 %all-gather.3.cloned.1.call-start = ((), (), s32[]{:S(2)}) async-start(), calls=%async_computation.2 | async-start | bytes 9437184 | tf_op jit(solution)/shard_map/all_gather | solution.py:126
  79.5 53.8 %copy-start.7 = (s32[1,1,2]{2,1,0:T(1,128)S(1)}, s32[1,1,2]{2,1,0:T(1,128)}, u32[]{:S(2)}) copy-start(s32[1,1,2]{2,1,0:T(1,128)} %param.11) | copy-start | bytes 28
  120.3 4.4 %copy-start.1 = (f32[2,512,256]{1,2,0:T(8,128)S(1)}, f32[2,512,256]{1,2,0:T(8,128)}, u32[]{:S(2)}) copy-start(f32[2,512,256]{1,2,0:T(8,128)} %get-tuple-element.294) | copy-start | bytes 3145732 | tf_op jit(solution)/shard_map/while
  124.7 3.6 %copy-start.2 = (f32[2,512,256]{2,1,0:T(8,128)S(1)}, f32[2,512,256]{2,1,0:T(8,128)}, u32[]{:S(2)}) copy-start(f32[2,512,256]{2,1,0:T(8,128)} %get-tuple-element.279) | copy-start | bytes 3145732 | tf_op jit(solution)/shard_map/while
  133.2 191.7 %reduce-scatter.4.cloned.1.call-start = ((), (), s32[]{:S(2)}) async-start(), calls=%async_computation.3 | async-start | bytes 2621440
  281.2 49.5 %copy-start.4 = (bf16[2,32,64,256]{3,2,1,0:T(8,128)(2,1)S(1)}, bf16[2,32,64,256]{3,2,1,0:T(8,128)(2,1)}, u32[]{:S(2)}) copy-start(bf16[2,32,64,256]{3,2,1,0:T(8,128)(2,1)} %param.9) | copy-start | bytes 6291460
Sparse Core Ops, SparseCore 0:
  19.0 59.4 all-reduce.4
  133.3 123.6 all-gather.2
  281.3 43.6 reduce-scatter.3
